TPU v7x, 32 devices: a whole 2x2x4 slice. The times are simulated.
32 devices in a mesh: rve: 4 (over y, x), slab: 8 (over z, core).
Axes of the slice: x: 2, y: 2, z: 4, core: 2. Of those that a mesh axis runs over, the one named last changes fastest.
Arguments:
- plastic_strain: float32 [6, 4, 96, 9216], P(None, 'rve', 'slab'), may hold values from -2 to 2
- hardening_var: float32 [4, 96, 9216], P('rve', 'slab'), may hold values from 0 to 1
- strain_start: float32 [6, 4, 96, 9216], P(None, 'rve', 'slab'), may hold values from -6 to 6
- strain_step: float32 [6, 4, 96, 9216], P(None, 'rve', 'slab'), may hold values from -4 to 4
- shear_mod: float32 [4, 96, 9216], P('rve', 'slab'), may hold values from 0.5 to 2
- bulk_mod: float32 [4, 96, 9216], P('rve', 'slab'), may hold values from 1 to 4
- yield_stress: float32 [4, 96, 9216], P('rve', 'slab'), may hold values from 0.5 to 4
- substeps: int32 [4, 384], replicated, may hold values from 1 to 8, as said below
- pull_group: int32 [4, 16], replicated, may hold values from 0 to 3, as said below
- pull_block: int32 [4, 16], replicated, may hold values from 0 to 383, as said below
- owner: int32 [4], replicated, may hold values from 0 to 3
Outputs:
- correction: float32 [3, 4, 96, 9216], P(None, 'rve', 'slab')
- inbox: float32 [7, 4, 16, 2304], P(None, 'rve', 'slab')
- element_sums: float32 [4, 42], P('rve')
Inputs may be any that keep to these rules, and one draw needn't show every extreme that they name: `substeps`: every RVE has a block with exactly its largest count, and some RVE reaches 8. `pull_group`: for each group g and each slab s, the 2 slots k with k // 2 = s name distinct source groups. `pull_block`: slot k names a block of z-slab k // 2: an id from (k // 2) * 4 * 12 to (k // 2 + 1) * 4 * 12 - 1.
All inputs are finite; a program needn't handle non-finite values.
Results may differ from a plain program's by a relative error of at most 0.0003.
Values sent between devices are 32-bit elements; how exact they have to be, the bound alone decides.
A program may use at most 192 MiB of HBM per device.

v0:
```python
import math

import jax
import jax.numpy as jnp
from jax import lax
from jax.sharding import PartitionSpec as P

NVX = 96
ITERS = 5
PLANE = 9216
BLK = 2304


hard_ratio = 0.3
mass_weight = 0.05
root_two_thirds = math.sqrt(2.0 / 3.0)
half_root = 1.0 / math.sqrt(2.0)


def with_halo(block, sides, width):
    for axis, dim in sides:
        count = lax.axis_size(axis)
        forward = [(i, i + 1) for i in range(count - 1)]
        forward.append((count - 1, 0))
        backward = [(target, source) for source, target in forward]
        low = lax.ppermute(
            lax.slice_in_dim(block, block.shape[dim] - width, None, axis=dim), axis, forward
        )
        high = lax.ppermute(lax.slice_in_dim(block, 0, width, axis=dim), axis, backward)
        block = jnp.concatenate([low, block, high], axis=dim)
    return block


def stencil_offsets():
    listing = []
    for depth_step in (-1, 0, 1):
        for row_step in (-1, 0, 1):
            for column_step in (-1, 0, 1):
                reach = abs(depth_step) + abs(row_step) + abs(column_step)
                if reach > 0:
                    listing.append((depth_step, row_step, column_step, (1.0, 0.5, 0.25)[reach - 1]))
    return listing


def plane_shift(values, row_step, column_step):
    if row_step != 0:
        values = jnp.roll(values, -row_step * NVX, axis=-1)
    if column_step != 0:
        column = jnp.arange(PLANE) % NVX
        plain = jnp.roll(values, -column_step, axis=-1)
        wrapped = jnp.roll(values, column_step * NVX - column_step, axis=-1)
        border = NVX - 1 if column_step > 0 else 0
        values = jnp.where(column == border, wrapped, plain)
    return values


def trace_vector(ndim):
    return jnp.array([1.0, 1.0, 1.0, 0.0, 0.0, 0.0], jnp.float32).reshape((6,) + (1,) * (ndim - 1))


def deviator_of(strain, plastic):
    elastic = strain - plastic
    volume = elastic[0] + elastic[1] + elastic[2]
    return (elastic - volume / 3.0 * trace_vector(strain.ndim), volume)


def return_map(
    plastic,
    hardening,
    strain_begin,
    strain_delta,
    shear_field,
    bulk_field,
    yield_field,
    count,
    turns,
):
    harden = hard_ratio * shear_field

    def substep(turn, carry):
        plastic_now, hardening_now, increment, direction, floored = carry
        turn_float = jnp.asarray(turn).astype(jnp.float32)
        strain = strain_begin + (turn_float + 1.0) / count * strain_delta
        deviator, volume = deviator_of(strain, plastic_now)
        trial = 2.0 * shear_field * deviator
        magnitude = jnp.sqrt(jnp.sum(trial * trial, axis=0))
        excess = magnitude - root_two_thirds * (yield_field + harden * hardening_now)
        active = turn_float < count
        new_increment = jnp.maximum(excess, 0.0) / (2.0 * shear_field + 2.0 / 3.0 * harden)
        new_floored = jnp.maximum(magnitude, root_two_thirds * yield_field)
        new_direction = trial / new_floored
        new_increment = jnp.where(active, new_increment, 0.0)
        plastic_now = plastic_now + new_increment * new_direction
        hardening_now = hardening_now + root_two_thirds * new_increment
        increment = jnp.where(active, new_increment, increment)
        direction = jnp.where(active, new_direction, direction)
        floored = jnp.where(active, new_floored, floored)
        return (plastic_now, hardening_now, increment, direction, floored)

    start = (
        plastic,
        hardening,
        jnp.zeros_like(hardening),
        jnp.zeros_like(plastic),
        jnp.ones_like(hardening),
    )
    plastic_new, hardening_new, increment, direction, floored = lax.fori_loop(
        0, turns, substep, start
    )
    deviator, volume = deviator_of(strain_begin + strain_delta, plastic_new)
    stress = bulk_field * volume * trace_vector(plastic.ndim) + 2.0 * shear_field * deviator
    theta = 1.0 - 2.0 * shear_field * increment / floored
    coefficient = shear_field * theta
    weight = shear_field * (theta - 1.0)
    return (stress, coefficient, plastic_new, hardening_new, weight, direction)


def rhs_from(stress, depth_diff):
    row_diff = 0.5 * (plane_shift(stress, 1, 0) - plane_shift(stress, -1, 0))
    column_diff = 0.5 * (plane_shift(stress, 0, 1) - plane_shift(stress, 0, -1))
    return jnp.stack(
        [
            column_diff[0] + half_root * (row_diff[5] + depth_diff[4]),
            half_root * (column_diff[5] + depth_diff[3]) + row_diff[1],
            half_root * (column_diff[4] + row_diff[3]) + depth_diff[2],
        ]
    )


def operate(field, coef_pad):
    depth = field.shape[1]
    padded = with_halo(field, (("slab", 1),), 1)
    coefficient = coef_pad[1 : depth + 1]
    total = mass_weight * coefficient * field
    for depth_step, row_step, column_step, weight in stencil_offsets():
        other = plane_shift(
            padded[:, 1 + depth_step : 1 + depth_step + depth], row_step, column_step
        )
        other_coef = plane_shift(
            coef_pad[1 + depth_step : 1 + depth_step + depth], row_step, column_step
        )
        total = total + 0.5 * weight * (coefficient + other_coef) * (field - other)
    return total


def finish(sums):
    trace_vec = jnp.array([1.0, 1.0, 1.0, 0.0, 0.0, 0.0], jnp.float32)
    outer = trace_vec[:, None] * trace_vec[None, :]
    projector = jnp.eye(6, dtype=jnp.float32) - outer / 3.0
    tangent = sums[6] * outer + 2.0 * sums[7] * projector + 2.0 * sums[8:].reshape(6, 6)
    return jnp.concatenate([sums[:6], tangent.reshape(36)])


def on_device(
    plastic_strain,
    hardening_var,
    strain_start,
    strain_step,
    shear_mod,
    bulk_mod,
    yield_stress,
    substeps,
    pull_group,
    pull_block,
    owner,
):
    groups = lax.axis_size("rve")
    slab_count = lax.axis_size("slab")
    group_index = lax.axis_index("rve")
    slab_index = lax.axis_index("slab")
    depth = plastic_strain.shape[2]
    cells = depth * PLANE
    blocks_dev = 4 * depth
    volume = float(depth * slab_count * PLANE)
    plastic = plastic_strain.reshape(6, cells)
    hardening = hardening_var.reshape(cells)
    begin = strain_start.reshape(6, cells)
    delta = strain_step.reshape(6, cells)
    shear_field = shear_mod.reshape(cells)
    bulk_field = bulk_mod.reshape(cells)
    yield_field = yield_stress.reshape(cells)
    local_costs = lax.dynamic_slice(
        substeps, (group_index, slab_index * blocks_dev), (1, blocks_dev)
    ).reshape(blocks_dev)
    count = jnp.broadcast_to(local_costs.astype(jnp.float32)[:, None], (blocks_dev, BLK)).reshape(
        cells
    )
    stress, coefficient, plastic_new, hardening_new, weight, direction = return_map(
        plastic,
        hardening,
        begin,
        delta,
        shear_field,
        bulk_field,
        yield_field,
        count,
        jnp.max(local_costs),
    )
    coupling = jnp.dot(weight[None, :] * direction, direction.T, precision=lax.Precision.HIGHEST)
    partial_value = (
        jnp.concatenate(
            [
                jnp.sum(stress, axis=1),
                jnp.sum(bulk_field)[None],
                jnp.sum(coefficient)[None],
                coupling.reshape(36),
            ]
        )
        / volume
    )
    in_dev = pull_group.shape[1] // slab_count
    slab_pulls = lax.dynamic_slice_in_dim(pull_group, slab_index * in_dev, in_dev, 1)
    slab_blocks = lax.dynamic_slice_in_dim(pull_block, slab_index * in_dev, in_dev, 1)
    match = slab_pulls == group_index
    wanted = jnp.any(match, axis=1)
    chosen = jnp.sum(jnp.where(match, slab_blocks - slab_index * blocks_dev, 0), axis=1)
    mine_source = lax.dynamic_index_in_dim(slab_pulls, group_index, 0, keepdims=False)
    history_new = jnp.concatenate([plastic_new, hardening_new[None]], axis=0)
    blocks = history_new.reshape(history_new.shape[0], blocks_dev, BLK)
    picked = jnp.take(blocks, chosen, axis=1)
    arrived = lax.all_to_all(
        jnp.where(wanted[None, :, None], picked, 0.0),
        "rve",
        split_axis=1,
        concat_axis=1,
        tiled=True,
    )
    inbox = jnp.take(arrived, mine_source, axis=1).reshape(arrived.shape[0], in_dev * BLK)
    stacked = jnp.concatenate([stress, coefficient[None]], axis=0).reshape(7, depth, PLANE)
    padded = with_halo(stacked, (("slab", 1),), 1)
    stress_pad = padded[:6]
    coef_pad = padded[6]
    rhs = rhs_from(stress_pad[:, 1:-1], 0.5 * (stress_pad[:, 2:] - stress_pad[:, :-2]))
    image = operate(rhs, coef_pad)
    rve_sums = lax.psum(partial_value, "slab")
    norm_now, curve_now = lax.psum((jnp.sum(rhs * rhs), jnp.sum(rhs * image)), "slab")
    solution = jnp.zeros_like(rhs)
    residual = rhs
    direction_cg = rhs
    alpha = norm_now / curve_now
    along = image
    for turn in range(ITERS):
        solution = solution + alpha * direction_cg
        residual = residual - alpha * along
        if turn + 1 < ITERS:
            image = operate(residual, coef_pad)
            norm_next, product = lax.psum(
                (jnp.sum(residual * residual), jnp.sum(residual * image)), "slab"
            )
            ratio = norm_next / norm_now
            alpha = norm_next / (product - ratio * norm_next / alpha)
            direction_cg = residual + ratio * direction_cg
            along = image + ratio * along
            norm_now = norm_next
    summary = finish(rve_sums)
    target = lax.dynamic_index_in_dim(owner, group_index, 0, keepdims=False)
    table = jnp.where((jnp.arange(groups) == target)[:, None], summary[None, :], 0.0)
    element_sums = lax.psum_scatter(table, "rve", scatter_dimension=0, tiled=True)
    return (solution.reshape(3, 1, depth, PLANE), inbox.reshape(7, 1, in_dev, BLK), element_sums)


def solution(mesh):
    return jax.shard_map(
        on_device,
        mesh=mesh,
        in_specs=(
            P(None, "rve", "slab", None),
            P("rve", "slab", None),
            P(None, "rve", "slab", None),
            P(None, "rve", "slab", None),
            P("rve", "slab", None),
            P("rve", "slab", None),
            P("rve", "slab", None),
            P(),
            P(),
            P(),
            P(),
        ),
        out_specs=(P(None, "rve", "slab", None), P(None, "rve", "slab", None), P("rve", None)),
        check_vma=False,
    )
```

profile of v0, /device:TPU:0, one launch (start us, length us, event | category | flops | bytes accessed | tf_op | source)
XLA Modules:
  0.0 1013.8 jit_solution(1216669223805341764)
XLA Ops:
  6.5 9.9 reduce.4
  20.0 10.4 %reduce.2 = f32[6,12,9216]{2,1,0:T(8,128)} reduce(f32[6,1,12,9216]{3,1,2,0:T(1,128)} %param.19, f32[]{:T(128)} %constant.692), dimensions={1}, to_apply=%param.19.reduce_sub_computation | reduce | bytes 5308420 | tf_op args[2]
  30.4 5.4 copy.22
  35.8 10.0 reduce.3
  45.8 5.6 copy.23
  56.4 144.6 %while.20 = (s32[]{:T(128)}, f32[6,110592]{1,0:T(8,128)S(1)}, f32[110592]{0:T(1024)}, f32[110592]{0:T(1024)}, f32[6,110592]{1,0:T(8,128)}, /*index=5*/f32[110592...) while((s32[]{:T(128)}, f32[6,110592]{1,0:T(8,128)S(1)}, ...), condition=%wide.region_3.4_spmd.clone.clone, body=%wide.region_1.3_spmd.sunk.clone.clone.sunk | while | flops 12275716 | bytes 83497744 | solution.py:107
  209.7 24.8 %all-to-all-start = ((f32[7,4,2304]{2,0,1:T(8,128)}), f32[7,4,2304]{2,0,1:T(8,128)}, u32[]{:S(2)}, u32[]{:S(2)}) async-start(f32[7,4,2304]{2,0,1:T(8,128)} %select_bitcast_fusion), calls=%async_computation | async-start | bytes 589824 | tf_op jit(solution)/shard_map/all_to_all | solution.py:221
  234.5 5.6 add_subtract_fusion.1
  290.8 7.7 fusion.4
  309.4 6.0 fusion.11
  398.5 64.0 %multiply_reduce_fusion.8 = (f32[]{:T(128)}, f32[]{:T(128)}, f32[3,12,9216]{2,1,0:T(8,128)}) fusion(f32[1,12,9216]{2,1,0:T(8,128)} %copy-done.13, f32[1,12,9216]{2,1,0:T(8,128)} %copy-done.15, f32[1,12,9216]{2,1,0:T(8,128)} %copy-done.11, f32[3,1,9216]{2,1,0:T(1,128)} %copy-done.88, f32[3,12,9215]{2,1,0:T(8,128)} %get-tuple-element.678, ...), kind=kLoop, calls=%fused_computation.1043 | loop fusion | flops 98537472 | bytes 73009160 | tf_op jit(solution)/shard_map/reduce_sum | solution.py:236
  462.5 14.7 %all-reduce.5 = (f32[]{:T(128)}, f32[]{:T(128)}) all-reduce(f32[]{:T(128)} %get-tuple-element.171, f32[]{:T(128)} %get-tuple-element.170), channel_id=1, replica_groups=mesh['rve'=4,'slab'=8] {'slab'}, use_global_device_ids=true, to_apply=%region_5.6 | all-reduce | flops 2 | bytes 16 | tf_op jit(solution)/shard_map/psum | solution.py:236
  533.7 53.8 %multiply_reduce_fusion.6 = (f32[]{:T(128)}, f32[]{:T(128)}, f32[3,12,9216]{2,1,0:T(8,128)}) fusion(f32[3,12,9216]{2,1,0:T(8,128)S(1)} %multiply_subtract_fusion.3, f32[3,1,9216]{2,1,0:T(1,128)} %copy-done.70, f32[3,12,9215]{2,1,0:T(8,128)} %get-tuple-element.458, f32[3,12,9121]{2,1,0:T(8,128)} %get-tuple-element.456, f32[3,12,95]{2,1,0:T(8,128)} %get-tuple-element.379, ...), kind=kLoop, calls=%fused_computation.1040 | loop fusion | flops 51093504 | bytes 70548200 | tf_op jit(solution)/shard_map/reduce_sum | solution.py:248
  587.5 18.3 %all-reduce.4 = (f32[]{:T(128)}, f32[]{:T(128)}) all-reduce(f32[]{:T(128)} %get-tuple-element.169, f32[]{:T(128)} %get-tuple-element.168), channel_id=1, replica_groups=mesh['rve'=4,'slab'=8] {'slab'}, use_global_device_ids=true, to_apply=%region_9.10 | all-reduce | flops 2 | bytes 16 | tf_op jit(solution)/shard_map/psum | solution.py:247
  661.1 5.2 fusion.267
  666.3 53.1 %multiply_reduce_fusion.4 = (f32[]{:T(128)}, f32[]{:T(128)}, f32[3,12,9216]{2,1,0:T(8,128)}) fusion(f32[3,12,9216]{2,1,0:T(8,128)S(1)} %multiply_subtract_fusion.2, f32[3,1,9216]{2,1,0:T(1,128)} %copy-done.71, f32[3,12,9215]{2,1,0:T(8,128)} %get-tuple-element.442, f32[3,12,9121]{2,1,0:T(8,128)} %get-tuple-element.440, f32[3,12,95]{2,1,0:T(8,128)} %get-tuple-element.345, ...), kind=kLoop, calls=%fused_computation.1036 | loop fusion | flops 51093504 | bytes 70548200 | tf_op jit(solution)/shard_map/reduce_sum | solution.py:248
  719.4 18.2 %all-reduce.3 = (f32[]{:T(128)}, f32[]{:T(128)}) all-reduce(f32[]{:T(128)} %get-tuple-element.167, f32[]{:T(128)} %get-tuple-element.166), channel_id=1, replica_groups=mesh['rve'=4,'slab'=8] {'slab'}, use_global_device_ids=true, to_apply=%region_13.14 | all-reduce | flops 2 | bytes 16 | tf_op jit(solution)/shard_map/psum | solution.py:247
  793.9 5.2 fusion.246
  799.1 53.2 %multiply_reduce_fusion.2 = (f32[]{:T(128)}, f32[]{:T(128)}, f32[3,12,9216]{2,1,0:T(8,128)}) fusion(f32[3,12,9216]{2,1,0:T(8,128)S(1)} %get-tuple-element.223, f32[3,1,9216]{2,1,0:T(1,128)} %copy-done.72, f32[3,12,9215]{2,1,0:T(8,128)} %get-tuple-element.426, f32[3,12,9121]{2,1,0:T(8,128)} %get-tuple-element.424, f32[3,12,95]{2,1,0:T(8,128)} %get-tuple-element.311, ...), kind=kLoop, calls=%fused_computation.1032 | loop fusion | flops 51093504 | bytes 70548200 | tf_op jit(solution)/shard_map/reduce_sum | solution.py:248
  852.4 18.0 %all-reduce.2 = (f32[]{:T(128)}, f32[]{:T(128)}) all-reduce(f32[]{:T(128)} %get-tuple-element.165, f32[]{:T(128)} %get-tuple-element.164), channel_id=1, replica_groups=mesh['rve'=4,'slab'=8] {'slab'}, use_global_device_ids=true, to_apply=%region_17.18 | all-reduce | flops 2 | bytes 16 | tf_op jit(solution)/shard_map/psum | solution.py:247
  925.5 5.4 fusion.221
  930.9 41.3 %fusion.18 = f32[]{:T(128)} fusion(f32[3,12,9216]{2,1,0:T(8,128)} %copy-done, f32[3,12,96]{2,1,0:T(8,128)} %copy-done.92, f32[3,12,96]{2,1,0:T(8,128)} %copy-done.94, f32[3,12,96]{2,1,0:T(8,128)} %copy-done.93, f32[3,12,96]{2,1,0:T(8,128)} %copy-done.91, f32[3,1,9216]{2,1,0:T(1,128)} %copy-done.74, f32[3,1,9216]{2,1,0:T(1,128)} %copy-done.73, ...), kind=kLoop, calls=%fused_computation.284 | loop fusion | flops 50429952 | bytes 69221088 | tf_op jit(solution)/shard_map/reduce_sum | solution.py:248
  972.1 18.0 %all-reduce.1 = (f32[]{:T(128)}, f32[]{:T(128)}, f32[44]{0:T(128)S(1)}) all-reduce(f32[]{:T(128)} %get-tuple-element.220, f32[]{:T(128)} %fusion.18, f32[44]{0:T(128)S(1)} %copy-done.126), channel_id=1, replica_groups=mesh['rve'=4,'slab'=8] {'slab'}, use_global_device_ids=true, to_apply=%region_21.22 | all-reduce | flops 46 | bytes 368 | tf_op jit(solution)/shard_map/psum | solution.py:247
  1002.4 10.1 all-reduce
  (721 shorter events, 523.4 us)
Async XLA Ops:
  209.7 105.8 %all-to-all-start = ((f32[7,4,2304]{2,0,1:T(8,128)}), f32[7,4,2304]{2,0,1:T(8,128)}, u32[]{:S(2)}, u32[]{:S(2)}) async-start(f32[7,4,2304]{2,0,1:T(8,128)} %select_bitcast_fusion), calls=%async_computation | async-start | bytes 589824 | tf_op jit(solution)/shard_map/all_to_all | solution.py:221
  257.4 60.5 %collective-permute-start = (f32[7,1,9216]{2,1,0:T(1,128)}, f32[7,1,9216]{2,1,0:T(1,128)}, u32[]{:S(2)}, u32[]{:S(2)}) collective-permute-start(f32[7,1,9216]{2,1,0:T(1,128)} %get-tuple-element.241), channel_id=1, source_target_pairs={{1,0},{2,1},{3,2},{4,3},{5,4},{6,5},{7,6},{0,7},{9,8},{10,9},{11,1... | collective-permute-start | bytes 774152 | tf_op jit(solution)/shard_map/ppermute | solution.py:29
  260.2 57.8 %collective-permute-start.1 = (f32[7,1,9216]{2,1,0:T(1,128)}, f32[7,1,9216]{2,1,0:T(1,128)}, u32[]{:S(2)}, u32[]{:S(2)}) collective-permute-start(f32[7,1,9216]{2,1,0:T(1,128)} %get-tuple-element.242), channel_id=1, source_target_pairs={{0,1},{1,2},{2,3},{3,4},{4,5},{5,6},{6,7},{7,0},{8,9},{9,10},{10,1... | collective-permute-start | bytes 774152 | tf_op jit(solution)/shard_map/ppermute | solution.py:26
  330.0 54.5 %copy-start.11 = (f32[1,12,9216]{2,1,0:T(8,128)}, f32[1,12,9216]{2,1,0:T(8,128)S(1)}, u32[]{:S(2)}) copy-start(f32[1,12,9216]{2,1,0:T(8,128)S(1)} %get-tuple-element.236) | copy-start | bytes 1327108
  330.0 54.5 %copy-start.13 = (f32[1,12,9216]{2,1,0:T(8,128)}, f32[1,12,9216]{2,1,0:T(8,128)S(1)}, u32[]{:S(2)}) copy-start(f32[1,12,9216]{2,1,0:T(8,128)S(1)} %get-tuple-element.237) | copy-start | bytes 1327108
  330.1 54.5 %copy-start.15 = (f32[1,12,9216]{2,1,0:T(8,128)}, f32[1,12,9216]{2,1,0:T(8,128)S(1)}, u32[]{:S(2)}) copy-start(f32[1,12,9216]{2,1,0:T(8,128)S(1)} %get-tuple-element.238) | copy-start | bytes 1327108
  347.5 17.3 %collective-permute-start.2 = (f32[3,1,9216]{2,1,0:T(1,128)S(1)}, f32[3,1,9216]{2,1,0:T(1,128)S(1)}, u32[]{:S(2)}, u32[]{:S(2)}) collective-permute-start(f32[3,1,9216]{2,1,0:T(1,128)S(1)} %get-tuple-element.643), channel_id=1, source_target_pairs={{0,1},{1,2},{2,3},{3,4},{4,5},{5,6},{6,7},{7,0},{8,9},{9,10},{10,1... | collective-permute-start | bytes 331784 | tf_op jit(solution)/shard_map/ppermute | solution.py:26
  347.6 17.2 %collective-permute-start.3 = (f32[3,1,9216]{2,1,0:T(1,128)S(1)}, f32[3,1,9216]{2,1,0:T(1,128)S(1)}, u32[]{:S(2)}, u32[]{:S(2)}) collective-permute-start(f32[3,1,9216]{2,1,0:T(1,128)S(1)} %get-tuple-element.644), channel_id=1, source_target_pairs={{1,0},{2,1},{3,2},{4,3},{5,4},{6,5},{7,6},{0,7},{9,8},{10,9},{11,1... | collective-permute-start | bytes 331784 | tf_op jit(solution)/shard_map/ppermute | solution.py:29
  480.8 6.0 collective-permute-start.4
  480.9 6.0 collective-permute-start.5
  533.6 76.6 %copy-start.12 = (f32[1,12,9216]{2,1,0:T(8,128)S(1)}, f32[1,12,9216]{2,1,0:T(8,128)}, u32[]{:S(2)}) copy-start(f32[1,12,9216]{2,1,0:T(8,128)} %copy-done.11) | copy-start | bytes 1327108
  533.6 76.6 %copy-start.14 = (f32[1,12,9216]{2,1,0:T(8,128)S(1)}, f32[1,12,9216]{2,1,0:T(8,128)}, u32[]{:S(2)}) copy-start(f32[1,12,9216]{2,1,0:T(8,128)} %copy-done.13) | copy-start | bytes 1327108
  533.6 76.6 %copy-start.16 = (f32[1,12,9216]{2,1,0:T(8,128)S(1)}, f32[1,12,9216]{2,1,0:T(8,128)}, u32[]{:S(2)}) copy-start(f32[1,12,9216]{2,1,0:T(8,128)} %copy-done.15) | copy-start | bytes 1327108
  612.8 6.0 collective-permute-start.6
  612.9 6.0 collective-permute-start.7
  618.8 42.3 %copy-start.68 = (f32[3,1,9216]{2,1,0:T(1,128)}, f32[3,1,9216]{2,1,0:T(1,128)S(1)}, u32[]{:S(2)}) copy-start(f32[3,1,9216]{2,1,0:T(1,128)S(1)} %collective-permute-done.6) | copy-start | bytes 331780
  618.8 42.3 %copy-start.71 = (f32[3,1,9216]{2,1,0:T(1,128)}, f32[3,1,9216]{2,1,0:T(1,128)S(1)}, u32[]{:S(2)}) copy-start(f32[3,1,9216]{2,1,0:T(1,128)S(1)} %collective-permute-done.7) | copy-start | bytes 331780
  745.9 6.0 collective-permute-start.8
  746.0 6.0 collective-permute-start.9
  751.9 42.0 %copy-start.69 = (f32[3,1,9216]{2,1,0:T(1,128)}, f32[3,1,9216]{2,1,0:T(1,128)S(1)}, u32[]{:S(2)}) copy-start(f32[3,1,9216]{2,1,0:T(1,128)S(1)} %collective-permute-done.8) | copy-start | bytes 331780
  751.9 42.0 %copy-start.72 = (f32[3,1,9216]{2,1,0:T(1,128)}, f32[3,1,9216]{2,1,0:T(1,128)S(1)}, u32[]{:S(2)}) copy-start(f32[3,1,9216]{2,1,0:T(1,128)S(1)} %collective-permute-done.9) | copy-start | bytes 331780
  877.4 48.1 %copy-start = (f32[3,12,9216]{2,1,0:T(8,128)}, f32[3,12,9216]{2,1,0:T(8,128)S(1)}, u32[]{:S(2)}) copy-start(f32[3,12,9216]{2,1,0:T(8,128)S(1)} %get-tuple-element.221) | copy-start | bytes 3981316
  877.5 6.0 collective-permute-start.10
  877.6 6.0 collective-permute-start.11
  (196 other events, 1158.1 us)
where the time goes:
time: 1030 us; the launch traced here: 1010 us
  other arithmetic  624 us (61%)
  local copies, waits for them, and re-layouts  205 us (20%)
  blocking collectives  97.3 us (9%)
  starting transfers between devices  46.3 us (4%)
  between operations  20.1 us (2%)
    reduce_sum x4, other arithmetic, on_device(): jnp.sum(residual * image)  201 us
    concatenate x48, other arithmetic, plane_shift(): values = jnp.roll(values, -row_step * NVX, axis=-1)  100 us
    psum x4, blocking collectives, on_device(): lax.psum((jnp.sum(residual * residual), jnp.sum(residual * image)), 'slab')  72.5 us
    concatenate x33, other arithmetic, with_halo(): block = jnp.concatenate([low, block, high], axis=dim)  64.5 us
    reduce_sum x1, other arithmetic, on_device(): jnp.sum(rhs * image)  64 us
    slice x26, local copies, waits for them, and re-layouts, plane_shift(): wrapped = jnp.roll(values, column_step * NVX - column_step, axis=-1)  46.9 us
    slice x22, local copies, waits for them, and re-layouts, plane_shift(): plain = jnp.roll(values, -column_step, axis=-1)  43.8 us
    while x182, local copies, waits for them, and re-layouts  33.5 us
  transfers between devices with their start and end apart: 13, of which 4 were waited for; matrix products, arithmetic and copies ran while one was open for 9% of the time, Pallas kernels for 0%

commit v1 on v0

v1 whole, which is shorter than its diff:
```python
import functools
import math

import jax
import jax.numpy as jnp
from jax import lax
from jax.experimental import pallas as pl
from jax.experimental.pallas import tpu as pltpu
from jax.sharding import PartitionSpec as P

NVX = 96
ITERS = 5
PLANE = 9216
BLK = 2304
LANES = 128
QUAD = 384
CHUNK = 1152
MESH = pl.DeviceIdType.MESH

hard_ratio = 0.3
mass_weight = 0.05
root_two_thirds = math.sqrt(2.0 / 3.0)
half_root = 1.0 / math.sqrt(2.0)
KEPT = (0, 1, 3, 4, 5)
PAIRS = tuple((i, j) for i in range(5) for j in range(i, 5))


def lane_id(rows):
    return lax.broadcasted_iota(jnp.int32, (rows, LANES), 1)


def unpack_rows(value):
    rows = value.shape[0]
    lane = lane_id(rows)
    a, b, c = value[:, 0:128], value[:, 128:256], value[:, 256:384]
    plain = (
        a,
        pltpu.roll(jnp.where(lane >= 96, a, b), 32, 1),
        pltpu.roll(jnp.where(lane >= 64, b, c), 64, 1),
        pltpu.roll(c, 96, 1),
    )
    out = []
    for row in plain:
        halo = jnp.where(lane < 112, pltpu.roll(row, 96, 1), pltpu.roll(row, 32, 1))
        out.append(jnp.where(lane < 96, row, halo))
    return out


def pack_rows(rows4):
    t0, t1, t2, t3 = rows4
    lane = lane_id(t0.shape[0])
    r1, r2, r3 = pltpu.roll(t1, 96, 1), pltpu.roll(t2, 64, 1), pltpu.roll(t3, 32, 1)
    return (
        jnp.where(lane < 96, t0, r1),
        jnp.where(lane < 64, r1, r2),
        jnp.where(lane < 32, r2, r3),
    )


def material_kernel(
    depth, volume, in_dev,
    sub_ref, pg_ref, pb_ref, p_ref, h_ref, b_ref, d_ref, g_ref, k_ref, y_ref,
    st_ref, pick_ref, sum_ref,
    acc_ref, hist_ref,
):
    step = pl.program_id(0)
    group = lax.axis_index("rve")
    slab = lax.axis_index("slab")
    groups = pg_ref.shape[0]
    per_block = BLK // CHUNK
    quarter = step // per_block
    blocks_dev = 4 * depth

    @pl.when(step == 0)
    def _():
        acc_ref[...] = jnp.zeros_like(acc_ref)

    zrow = lax.broadcasted_iota(jnp.int32, (depth, LANES), 0)
    count = jnp.zeros((depth, LANES), jnp.int32)
    turns = jnp.int32(1)
    for z in range(depth):
        n = sub_ref[group, slab * blocks_dev + z * 4 + quarter]
        count = jnp.where(zrow == z, n, count)
        turns = jnp.maximum(turns, n)
    count = jnp.concatenate([count] * (QUAD // LANES), axis=1)
    waiting = turns - count
    inv = 1.0 / count.astype(jnp.float32)
    waiting_f = waiting.astype(jnp.float32)

    def dev_parts(ref, lanes, other=None):
        parts = []
        for c in range(6):
            v = ref[c, 0, :, lanes]
            if other is not None:
                v = v - other[c, 0, :, lanes]
            parts.append(v)
        trace = parts[0] + parts[1] + parts[2]
        third = trace * (1.0 / 3.0)
        return [parts[c] - third if c < 3 else parts[c] for c in range(6)], trace

    def sub_chunk(sc, _):
        off = pl.multiple_of(sc * QUAD, QUAD)
        lanes = pl.ds(off, QUAD)
        dev0, tr0 = dev_parts(b_ref, lanes, p_ref)
        devs, trs = dev_parts(d_ref, lanes)
        mu = g_ref[0, :, lanes]
        hard = h_ref[0, :, lanes]
        delta = [devs[c] * inv for c in KEPT]
        start = [dev0[c] - waiting_f * delta[i] for i, c in enumerate(KEPT)]
        level0 = (11.0 * root_two_thirds / 2.2) * (y_ref[0, :, lanes] / mu + hard_ratio * hard)

        def trial(dd):
            dd = [dd[i] + delta[i] for i in range(5)]
            square = (
                2.0 * (dd[0] * (dd[0] + dd[1]) + dd[1] * dd[1])
                + dd[2] * dd[2] + dd[3] * dd[3] + dd[4] * dd[4]
            )
            square = jnp.maximum(square, 1e-30)
            return dd, square, lax.rsqrt(square)

        def substep(turn, carry):
            dd, level = carry
            dd, square, rs = trial(dd)
            fac = jnp.minimum((1.0 + level * rs) * (1.0 / 11.0), 1.0)
            fac = jnp.where(turn >= waiting, fac, 1.0)
            level = level + (1.0 - fac) * (square * rs)
            return tuple(fac * v for v in dd), level

        dd, level = lax.fori_loop(0, turns - 1, substep, (tuple(start), level0))
        dd, square, rs = trial(dd)
        fac = jnp.minimum((1.0 + level * rs) * (1.0 / 11.0), 1.0)
        level = level + (1.0 - fac) * (square * rs)
        fin = [fac * v for v in dd]
        coef = mu * fac
        weight = (coef - mu) * (rs * rs)
        bulk = k_ref[0, :, lanes]
        vol = bulk * (tr0 + trs)
        two_mu = 2.0 * mu
        ms = [two_mu * v for v in fin]
        wn = [weight * v for v in dd]
        terms = [vol, bulk, coef] + ms + [wn[i] * dd[j] for i, j in PAIRS]
        for t, v in enumerate(terms):
            acc_ref[t] += v[:, 0:128] + v[:, 128:256] + v[:, 256:384]
        ms6 = [ms[0], ms[1], -(ms[0] + ms[1]), ms[2], ms[3], ms[4]]
        fin6 = [fin[0], fin[1], -(fin[0] + fin[1]), fin[2], fin[3], fin[4]]
        fields = [ms6[c] + vol if c < 3 else ms6[c] for c in range(6)] + [coef]
        row0 = (step * (CHUNK // QUAD) + sc) * 4
        for f, v in enumerate(fields):
            for r, rowv in enumerate(unpack_rows(v)):
                for z0 in range(0, depth, 8):
                    nz = min(8, depth - z0)
                    st_ref[f, pl.ds(z0 * NVX + row0 + r, nz, stride=NVX), :] = rowv[z0 : z0 + nz]
        for c in range(6):
            hist_ref[c, :, lanes] = p_ref[c, 0, :, lanes] + (dev0[c] + devs[c] - fin6[c])
        hist_ref[6, :, lanes] = hard + root_two_thirds * (level - level0)
        return 0

    lax.fori_loop(0, CHUNK // QUAD, sub_chunk, 0)

    for g in range(groups):
        chosen = jnp.int32(0)
        for j in range(in_dev):
            slot = slab * in_dev + j
            chosen = jnp.where(
                pg_ref[g, slot] == group, pb_ref[g, slot] - slab * blocks_dev, chosen
            )

        @pl.when(chosen % 4 == quarter)
        def _():
            z = chosen // 4
            lanes = pl.ds(pl.multiple_of((step % per_block) * CHUNK, CHUNK), CHUNK)
            for c in range(7):
                pick_ref[g, pl.ds(c, 1), lanes] = hist_ref[c, pl.ds(z, 1), :]

    @pl.when(step == pl.num_programs(0) - 1)
    def _():
        tot = [
            jnp.sum(acc_ref[t], axis=(0, 1), keepdims=True) * (1.0 / volume)
            for t in range(8 + len(PAIRS))
        ]
        vol, bulk, coef = tot[0], tot[1], tot[2]
        ms = tot[3:8]
        stress = [vol + ms[0], vol + ms[1], vol - ms[0] - ms[1], ms[2], ms[3], ms[4]]
        table = {}
        for t, (i, j) in enumerate(PAIRS):
            table[(KEPT[i], KEPT[j])] = tot[8 + t]
            table[(KEPT[j], KEPT[i])] = tot[8 + t]
        for j in KEPT:
            table[(2, j)] = -(table[(0, j)] + table[(1, j)])
            table[(j, 2)] = table[(2, j)]
        table[(2, 2)] = -(table[(2, 0)] + table[(2, 1)])
        lane = lane_id(1)
        row = jnp.zeros((1, LANES), jnp.float32)
        for c in range(6):
            row = jnp.where(lane == c, stress[c], row)
        for i in range(6):
            for j in range(6):
                v = 2.0 * table[(i, j)]
                if i == j:
                    v = v + 2.0 * coef
                if i < 3 and j < 3:
                    v = v + bulk - (2.0 / 3.0) * coef
                row = jnp.where(lane == 6 + 6 * i + j, v, row)
        sum_ref[...] = row


def spread(v):
    p = v + pltpu.roll(v, NVX - 1, 0)
    p = p + pltpu.roll(p, 1, 0)
    q = p + pltpu.roll(p, LANES - 1, 1)
    return q + pltpu.roll(q, 1, 1)


def fold(v):
    out = v[0:8]
    for i in range(1, NVX // 8):
        out = out + v[8 * i : 8 * i + 8]
    return out


def solve_kernel(
    depth, groups, slabs, in_dev,
    pg_ref, own_ref, st_ref, pick_ref, sum_ref,
    out_ref, inbox_ref, elem_ref,
    sh, c8, ee, rr, im, al, dd, uu, hb, ps, red, ab, es, eo,
    nsend, nrecv, rsend, rrecv, bsend, brecv, esend, erecv,
):
    group = lax.axis_index("rve")
    slab = lax.axis_index("slab")
    up = lax.rem(slab + 1, slabs)
    down = lax.rem(slab + slabs - 1, slabs)
    last = depth - 1

    barrier = pltpu.get_barrier_semaphore()
    for k in range(1, slabs):
        pl.semaphore_signal(
            barrier, inc=1, device_id={"slab": lax.rem(slab + k, slabs)}, device_id_type=MESH
        )
    for k in range(1, groups):
        pl.semaphore_signal(
            barrier, inc=1, device_id={"rve": lax.rem(group + k, groups)}, device_id_type=MESH
        )
    pl.semaphore_wait(barrier, slabs + groups - 2)

    def remote(src, dst, ssem, rsem, axis, to):
        return pltpu.make_async_remote_copy(
            src_ref=src, dst_ref=dst, send_sem=ssem, recv_sem=rsem,
            device_id={axis: to}, device_id_type=MESH,
        )

    stress_up = remote(st_ref.at[:, last], sh.at[0], nsend.at[0, 0], nrecv.at[0, 0], "slab", up)
    stress_down = remote(st_ref.at[:, 0], sh.at[1], nsend.at[0, 1], nrecv.at[0, 1], "slab", down)
    stress_up.start()
    stress_down.start()
    moves = []
    for k in range(1, groups):
        to = lax.rem(group + k, groups)
        move = remote(pick_ref.at[to], ab.at[group], bsend.at[k], brecv.at[k], "rve", to)
        move.start()
        moves.append(move)

    c8[0] = jnp.zeros((NVX, LANES), jnp.float32)

    def own_planes(z, _):
        c8[z + 1] = st_ref[6, z] * 0.125
        return 0

    lax.fori_loop(0, depth, own_planes, 0)
    ab[group] = pick_ref[group]

    def ydiff(v):
        return pltpu.roll(v, NVX - 1, 0) - pltpu.roll(v, 1, 0)

    def xdiff(v):
        return pltpu.roll(v, LANES - 1, 1) - pltpu.roll(v, 1, 1)

    def rhs_plane(z, below, above):
        s3, s4, s5 = st_ref[3, z], st_ref[4, z], st_ref[5, z]
        zd = {c: above(c) - below(c) for c in (2, 3, 4)}
        hr = 0.5 * half_root
        v0 = 0.5 * xdiff(st_ref[0, z]) + hr * (ydiff(s5) + zd[4])
        v1 = hr * (xdiff(s5) + zd[3]) + 0.5 * ydiff(st_ref[1, z])
        v2 = hr * (xdiff(s4) + ydiff(s3)) + 0.5 * zd[2]
        for c, v in enumerate((v0, v1, v2)):
            rr[c, z + 1] = v

    def rhs_inner(z, _):
        rhs_plane(z, lambda c: st_ref[c, z - 1], lambda c: st_ref[c, z + 1])
        return 0

    lax.fori_loop(1, last, rhs_inner, 0)
    stress_up.wait()
    stress_down.wait()
    rhs_plane(0, lambda c: sh[0, c], lambda c: st_ref[c, 1])
    rhs_plane(last, lambda c: st_ref[c, last - 1], lambda c: sh[1, c])
    r_up = remote(rr.at[:, depth], rr.at[:, 0], nsend.at[1, 0], nrecv.at[1, 0], "slab", up)
    r_down = remote(rr.at[:, 1], rr.at[:, depth + 1], nsend.at[1, 1], nrecv.at[1, 1], "slab", down)
    r_up.start()
    r_down.start()
    c8[0] = sh[0, 6] * 0.125
    c8[depth + 1] = sh[1, 6] * 0.125

    def diagonal(z, _):
        ee[z] = 8.0 * (8.0 + mass_weight) * c8[z] + spread(c8[z - 1] + 2.0 * c8[z] + c8[z + 1])
        return 0

    lax.fori_loop(1, depth + 1, diagonal, 0)

    zero = jnp.zeros((8, LANES), jnp.float32)

    def apply_plane(z, carry):
        norm, curve = carry
        ca, cb, cc = c8[z - 1], c8[z], c8[z + 1]
        diag = ee[z]
        for c in range(3):
            ra, rb, rc = rr[c, z - 1], rr[c, z], rr[c, z + 1]
            crb = cb * rb
            plain = spread((ra + rc) + (rb + rb))
            mixed = spread((ca * ra + cc * rc) + (crb + crb))
            image = diag * rb - cb * plain - mixed
            im[c, z] = image
            norm = norm + fold(rb * rb)
            curve = curve + fold(rb * image)
        return norm, curve

    def reduce_start(it, norm, curve, extra):
        row = lax.broadcasted_iota(jnp.int32, (8, LANES), 0)
        n = jnp.sum(norm, axis=0, keepdims=True)
        c = jnp.sum(curve, axis=0, keepdims=True)
        tile = jnp.where(row == 0, n, jnp.where(row == 1, c, 0.0))
        if extra is not None:
            tile = jnp.where(row == 2, extra, tile)
        ps[it] = tile
        copies = []
        for k in range(1, slabs):
            to = lax.rem(slab + k, slabs)
            copy = remote(ps.at[it], red.at[it, slab], rsend.at[it, k], rrecv.at[it, k], "slab", to)
            copy.start()
            copies.append(copy)
        red[it, slab] = tile
        return copies

    def reduce_end(it, copies):
        for copy in copies:
            copy.wait()
        total = red[it, 0]
        for k in range(1, slabs):
            total = total + red[it, k]
        kept = jnp.where(lane_id(8) < NVX, total, 0.0)
        sums = jnp.sum(kept, axis=1, keepdims=True)
        return total, sums[0:1], sums[1:2]

    carry = lax.fori_loop(2, depth, apply_plane, (zero, zero))
    r_up.wait()
    r_down.wait()
    carry = apply_plane(1, carry)
    carry = apply_plane(depth, carry)

    def send_image(it):
        first = remote(im.at[:, depth], hb.at[it, 0], nsend.at[2 + it, 0], nrecv.at[2 + it, 0], "slab", up)
        second = remote(im.at[:, 1], hb.at[it, 1], nsend.at[2 + it, 1], nrecv.at[2 + it, 1], "slab", down)
        first.start()
        second.start()
        return first, second

    halos = send_image(0)
    copies = reduce_start(0, *carry, sum_ref[...])
    total, norm_now, curve_now = reduce_end(0, copies)
    eo[...] = total
    element = []
    for k in range(1, groups):
        to = lax.rem(group + k, groups)
        copy = remote(eo, es.at[group], esend.at[k], erecv.at[k], "rve", to)
        copy.start()
        element.append(copy)
    es[group] = total
    alpha = norm_now / curve_now

    ratio = None
    for turn in range(ITERS - 1):
        for copy in halos:
            copy.wait()

        def refresh(c, z, fresh):
            if turn > 0:
                fresh = fresh + ratio * al[c, z]
            al[c, z] = fresh
            rr[c, z] = rr[c, z] - alpha * fresh

        for c in range(3):
            refresh(c, 0, hb[turn, 0, c])
            refresh(c, depth + 1, hb[turn, 1, c])

        def direction(z):
            rows = pl.ds(pl.multiple_of((z - 1) * NVX, NVX), NVX)
            for c in range(3):
                if turn == 0:
                    d = rr[c, z]
                    uu[c, rows, :] = alpha * d
                else:
                    d = rr[c, z] + ratio * dd[c, z - 1]
                    uu[c, rows, :] = uu[c, rows, :] + alpha * d
                dd[c, z - 1] = d

        def update(z, _):
            direction(z)
            for c in range(3):
                refresh(c, z, im[c, z])
            return 0

        lax.fori_loop(1, depth + 1, update, 0)
        carry = apply_plane(1, (zero, zero))
        carry = apply_plane(depth, carry)
        if turn + 1 < ITERS - 1:
            halos = send_image(turn + 1)
        carry = lax.fori_loop(2, depth, apply_plane, carry)
        copies = reduce_start(turn + 1, *carry, None)
        _, norm_next, product = reduce_end(turn + 1, copies)
        ratio = norm_next / norm_now
        alpha = norm_next / (product - ratio * norm_next / alpha)
        norm_now = norm_next

    def last_turn(z, _):
        rows = pl.ds(pl.multiple_of(z * NVX, NVX), NVX)
        for c in range(3):
            d = rr[c, z + 1] + ratio * dd[c, z]
            uu[c, rows, :] = uu[c, rows, :] + alpha * d
        return 0

    lax.fori_loop(0, depth, last_turn, 0)

    def to_flat(j, _):
        for c in range(3):
            for z0 in range(0, depth, 8):
                nz = min(8, depth - z0)
                rows4 = [
                    uu[c, pl.ds(z0 * NVX + 4 * j + r, nz, stride=NVX), :] for r in range(4)
                ]
                for t, v in enumerate(pack_rows(rows4)):
                    off = pl.multiple_of(j * QUAD + t * LANES, LANES)
                    out_ref[c, 0, pl.ds(z0, nz), pl.ds(off, LANES)] = v
        return 0

    lax.fori_loop(0, PLANE // QUAD, to_flat, 0)

    for move in moves:
        move.wait()
    for j in range(in_dev):
        source = pg_ref[group, slab * in_dev + j]
        got = ab[source]
        for c in range(7):
            inbox_ref[c, 0, pl.ds(j, 1), :] = got[c : c + 1]
    for copy in element:
        copy.wait()
    mine = jnp.zeros((1, LANES), jnp.float32)
    for k in range(groups):
        mine = mine + jnp.where(own_ref[k] == group, es[k][2:3], 0.0)
    elem_ref[...] = mine[:, 0:42]


def on_device(
    groups, slabs,
    plastic_strain, hardening_var, strain_start, strain_step, shear_mod, bulk_mod, yield_stress,
    substeps, pull_group, pull_block, owner,
):
    depth = plastic_strain.shape[2]
    in_dev = pull_group.shape[1] // slabs
    volume = float(depth * slabs * PLANE)
    smem = pl.BlockSpec(memory_space=pltpu.SMEM)
    vmem = pl.BlockSpec(memory_space=pltpu.VMEM)
    f32 = jnp.float32
    six = pl.BlockSpec((6, 1, depth, CHUNK), lambda i: (0, 0, 0, i))
    one = pl.BlockSpec((1, depth, CHUNK), lambda i: (0, 0, i))

    def whole(shape):
        return pl.BlockSpec(shape, lambda i: (0,) * len(shape))

    shapes = ((7, depth * NVX, LANES), (groups, 7, BLK), (1, LANES))
    stress, picked, partial_sums = pl.pallas_call(
        functools.partial(material_kernel, depth, volume, in_dev),
        grid=(PLANE // CHUNK,),
        in_specs=[smem, smem, smem, six, one, six, six, one, one, one],
        out_specs=[whole(s) for s in shapes],
        out_shape=[jax.ShapeDtypeStruct(s, f32) for s in shapes],
        scratch_shapes=[
            pltpu.VMEM((8 + len(PAIRS), depth, LANES), f32),
            pltpu.VMEM((7, depth, CHUNK), f32),
        ],
        compiler_params=pltpu.CompilerParams(
            dimension_semantics=("arbitrary",), vmem_limit_bytes=48 * 1024 * 1024
        ),
        name="material",
    )(
        substeps, pull_group, pull_block, plastic_strain, hardening_var, strain_start,
        strain_step, shear_mod, bulk_mod, yield_stress,
    )
    stress = stress.reshape(7, depth, NVX, LANES)
    plane = (NVX, LANES)
    dma = pltpu.SemaphoreType.DMA
    correction, inbox, element_sums = pl.pallas_call(
        functools.partial(solve_kernel, depth, groups, slabs, in_dev),
        in_specs=[smem, smem, vmem, vmem, vmem],
        out_specs=[vmem, vmem, vmem],
        out_shape=[
            jax.ShapeDtypeStruct((3, 1, depth, PLANE), f32),
            jax.ShapeDtypeStruct((7, 1, in_dev, BLK), f32),
            jax.ShapeDtypeStruct((1, 42), f32),
        ],
        scratch_shapes=[
            pltpu.VMEM((2, 7) + plane, f32),
            pltpu.VMEM((depth + 2,) + plane, f32),
            pltpu.VMEM((depth + 2,) + plane, f32),
            pltpu.VMEM((3, depth + 2) + plane, f32),
            pltpu.VMEM((3, depth + 2) + plane, f32),
            pltpu.VMEM((3, depth + 2) + plane, f32),
            pltpu.VMEM((3, depth) + plane, f32),
            pltpu.VMEM((3, depth * NVX, LANES), f32),
            pltpu.VMEM((ITERS - 1, 2, 3) + plane, f32),
            pltpu.VMEM((ITERS, 8, LANES), f32),
            pltpu.VMEM((ITERS, slabs, 8, LANES), f32),
            pltpu.VMEM((groups, 7, BLK), f32),
            pltpu.VMEM((groups, 8, LANES), f32),
            pltpu.VMEM((8, LANES), f32),
            dma((ITERS + 1, 2)),
            dma((ITERS + 1, 2)),
            dma((ITERS, slabs)),
            dma((ITERS, slabs)),
            dma((groups,)),
            dma((groups,)),
            dma((groups,)),
            dma((groups,)),
        ],
        compiler_params=pltpu.CompilerParams(
            collective_id=0, has_side_effects=True, vmem_limit_bytes=60 * 1024 * 1024
        ),
        name="solve",
    )(pull_group, owner, stress, picked, partial_sums)
    return correction, inbox, element_sums


def solution(mesh):
    return jax.shard_map(
        functools.partial(on_device, mesh.shape["rve"], mesh.shape["slab"]),
        mesh=mesh,
        in_specs=(
            P(None, "rve", "slab", None),
            P("rve", "slab", None),
            P(None, "rve", "slab", None),
            P(None, "rve", "slab", None),
            P("rve", "slab", None),
            P("rve", "slab", None),
            P("rve", "slab", None),
            P(),
            P(),
            P(),
            P(),
        ),
        out_specs=(P(None, "rve", "slab", None), P(None, "rve", "slab", None), P("rve", None)),
        check_vma=False,
    )
```

time: 1030 us -> 107 us (0.10); the launches traced: 1010 us -> 106 us
  other arithmetic: 624 us -> 0 us
  local copies, waits for them, and re-layouts: 205 us -> 16.5 us
  blocking collectives: 97.3 us -> 0 us
  Pallas kernels: 0 us -> 88.6 us
  starting transfers between devices: 46.3 us -> 0 us
  between operations: 20.1 us -> 0.73 us
    reduce_sum x17 -> x0, other arithmetic: 288 us -> none  [the longest x4 201 us: on_device(): jnp.sum(residual * image)]
    concatenate x83 -> x0, other arithmetic: 169 us -> none  [the longest x48 100 us: plane_shift(): values = jnp.roll(values, -row_step * NVX, axis=-1)]
    slice x67 -> x0, local copies, waits for them, and re-layouts: 103 us -> none  [the longest x26 46.9 us: plane_shift(): wrapped = jnp.roll(values, column_step * NVX - column_step, axis=-1)]
    pallas_call x0 -> x2, Pallas kernels: none -> 88.6 us  [the longest x1 68 us: on_device(): pl.pallas_call(functools.partial(solve_kernel, depth, groups, slabs, in_d...]
    psum x5 -> x0, blocking collectives: 87.2 us -> none  [the longest x4 72.5 us: on_device(): lax.psum((jnp.sum(residual * residual), jnp.sum(residual * image)), 'slab')]
    mul x19 -> x0, other arithmetic: 44.9 us -> none  [the longest x7 12.8 us: substep(): trial = 2.0 * shear_field * deviator]
    sub x11 -> x0, other arithmetic: 42 us -> none  [the longest x8 33.3 us: deviator_of(): elastic = strain - plastic]
    while x182 -> x0, local copies, waits for them, and re-layouts: 33.5 us -> none
  transfers between devices with their start and end apart: 13 -> 0, of which waited for: 4 -> 0; matrix products, arithmetic and copies ran while one was open for 9% -> 0% of each run, Pallas kernels for 0% -> 0%
where the time goes in v1:
time: 107 us; the launch traced here: 106 us
  Pallas kernels  88.6 us (83%)
  local copies, waits for them, and re-layouts  16.5 us (15%)
    pallas_call x1, Pallas kernels, on_device(): pl.pallas_call(functools.partial(solve_kernel, depth, groups, slabs, in_d...  68 us
    pallas_call x1, Pallas kernels, on_device(): pl.pallas_call(functools.partial(material_kernel, depth, volume, in_dev),...  20.7 us
    unnamed x31, local copies, waits for them, and re-layouts  12.5 us
    pallas_call x1, local copies, waits for them, and re-layouts, on_device(): pl.pallas_call(functools.partial(solve_kernel, depth, groups, slabs, in_d...  3.94 us

profile of v1, /device:TPU:0, one launch (start us, length us, event | category | flops | bytes accessed | tf_op | source)
XLA Modules:
  0.0 105.8 jit_solution(258268165047552975)
XLA Ops:
  0.6 0.0 copy-start.8
  0.6 0.0 copy-start.5
  0.7 1.3 %copy.15.h_ref = f32[1,12,9216]{2,1,0:T(8,128)S(1)} copy(f32[1,12,9216]{2,0,1:T(1,128)} %param.12) | data formatting | bytes 884736 | tf_op args[1]
  1.9 1.1 %copy.18.g_ref = f32[1,12,9216]{2,1,0:T(8,128)S(1)} copy(f32[1,12,9216]{2,0,1:T(1,128)} %param.15) | data formatting | bytes 884736 | tf_op args[4]
  3.0 1.1 %copy.19.k_ref = f32[1,12,9216]{2,1,0:T(8,128)S(1)} copy(f32[1,12,9216]{2,0,1:T(1,128)} %param.16) | data formatting | bytes 884736 | tf_op args[5]
  4.1 0.0 copy-done.8
  4.2 0.1 copy.20.y_ref
  4.3 0.0 copy-done.5
  4.3 0.0 copy-start.6
  4.3 0.5 copy.14.p_ref
  4.8 1.2 %copy-done.6 = f32[6,1,12,9216]{3,1,2,0:T(1,128)S(1)} copy-done((f32[6,1,12,9216]{3,1,2,0:T(1,128)S(1)}, f32[6,1,12,9216]{3,1,2,0:T(1,128)}, u32[]{:S(2)}) %copy-start.6) | copy-done | bytes 2654232
  6.0 2.3 %copy.16.b_ref = f32[6,1,12,9216]{3,2,1,0:T(8,128)} copy(f32[6,1,12,9216]{3,1,2,0:T(1,128)S(1)} %copy-done.6) | data formatting | bytes 5308416 | tf_op args[2]
  8.3 0.1 copy-done.7
  8.4 2.4 %copy.17.d_ref = f32[6,1,12,9216]{3,2,1,0:T(8,128)} copy(f32[6,1,12,9216]{3,1,2,0:T(1,128)S(1)} %copy-done.7) | data formatting | bytes 5308416 | tf_op args[3]
  10.8 0.0 copy-done.1
  10.8 0.0 copy-done.2
  10.8 20.7 %material.1 = (f32[7,1152,128]{2,1,0:T(8,128)}, f32[4,7,2304]{2,1,0:T(8,128)S(1)}, f32[1,128]{1,0:T(1,128)S(1)}) custom-call(s32[4,384]{1,0:T(4,128)S(1)} %copy-done.2, s32[4,16]{1,0:T(4,128)S(1)} %copy-done.1, s32[4,16]{1,0:T(4,128)S(1)} %copy-done.3, f32[6,1,12,9216]{3,2,1,0:T(8,128)S(1)} %copy.14.p_ref, f32[1,12,9216]{2,1,0:T(8,128)S(1)} %copy.15.h_ref, ...), custom_call_target="tpu_custom_call" | custom-call | tf_op jit(solution)/shard_map/material/pallas_call | solution.py:479
  31.5 0.7 copy-done
  32.2 0.5 copy-done.4
  32.7 68.0 %solve.1 = (f32[3,1,12,9216]{3,2,1,0:T(8,128)}, f32[7,1,2,2304]{3,2,1,0:T(2,128)}, f32[1,42]{1,0:T(1,128)}) custom-call(s32[4,16]{1,0:T(4,128)} %pg_ref.3, s32[4]{0:T(128)} %own_ref.1, f32[7,12,96,128]{3,2,1,0:T(8,128)} %bitcast.1, f32[4,7,2304]{2,1,0:T(8,128)} %copy-done, f32[1,128]{1,0:T(1,128)} %copy-done.4), custom_call_target="tpu_custom_call" | custom-call | tf_op jit(solution)/shard_map/solve/pallas_call | solution.py:500
  100.7 3.9 %copy.21 = f32[3,1,12,9216]{3,1,2,0:T(1,128)} copy(f32[3,1,12,9216]{3,2,1,0:T(8,128)} %get-tuple-element.9) | data formatting | bytes 2654208 | tf_op jit(solution)/shard_map/solve/pallas_call | solution.py:500
  104.7 0.0 copy-done.9
  104.7 0.7 copy.24
  105.3 0.5 copy.25
  (10 shorter events, 0.0 us)
Async XLA Ops:
  0.6 3.5 %copy-start.8 = (f32[1,12,9216]{2,0,1:T(1,128)S(1)}, f32[1,12,9216]{2,0,1:T(1,128)}, u32[]{:S(2)}) copy-start(f32[1,12,9216]{2,0,1:T(1,128)} %param.17) | copy-start | bytes 1327108
  0.6 3.6 %copy-start.5 = (f32[6,1,12,9216]{3,1,2,0:T(1,128)S(1)}, f32[6,1,12,9216]{3,1,2,0:T(1,128)}, u32[]{:S(2)}) copy-start(f32[6,1,12,9216]{3,1,2,0:T(1,128)} %param.11) | copy-start | bytes 7962628
  4.3 1.8 %copy-start.6 = (f32[6,1,12,9216]{3,1,2,0:T(1,128)S(1)}, f32[6,1,12,9216]{3,1,2,0:T(1,128)}, u32[]{:S(2)}) copy-start(f32[6,1,12,9216]{3,1,2,0:T(1,128)} %param.13) | copy-start | bytes 7962628
  6.0 2.4 %copy-start.7 = (f32[6,1,12,9216]{3,1,2,0:T(1,128)S(1)}, f32[6,1,12,9216]{3,1,2,0:T(1,128)}, u32[]{:S(2)}) copy-start(f32[6,1,12,9216]{3,1,2,0:T(1,128)} %param.14) | copy-start | bytes 7962628
  8.4 2.4 %copy-start.1 = (s32[4,16]{1,0:T(4,128)S(1)}, s32[4,16]{1,0:T(4,128)}, u32[]{:S(2)}) copy-start(s32[4,16]{1,0:T(4,128)} %pg_ref.3) | copy-start | bytes 772
  8.4 2.4 %copy-start.2 = (s32[4,384]{1,0:T(4,128)S(1)}, s32[4,384]{1,0:T(4,128)}, u32[]{:S(2)}) copy-start(s32[4,384]{1,0:T(4,128)} %sub_ref.1) | copy-start | bytes 18436
  8.4 2.4 %copy-start.3 = (s32[4,16]{1,0:T(4,128)S(1)}, s32[4,16]{1,0:T(4,128)}, u32[]{:S(2)}) copy-start(s32[4,16]{1,0:T(4,128)} %pb_ref.1) | copy-start | bytes 772
  31.5 0.7 copy-start
  32.2 0.5 copy-start.4
  100.7 4.0 %copy-start.9 = (f32[7,1,2,2304]{3,2,1,0:T(2,128)S(1)}, f32[7,1,2,2304]{3,2,1,0:T(2,128)}, u32[]{:S(2)}) copy-start(f32[7,1,2,2304]{3,2,1,0:T(2,128)} %get-tuple-element.16) | copy-start | bytes 387076
  100.7 4.6 %copy-start.10 = (f32[1,42]{1,0:T(1,128)S(1)}, f32[1,42]{1,0:T(1,128)}, u32[]{:S(2)}) copy-start(f32[1,42]{1,0:T(1,128)} %get-tuple-element.17) | copy-start | bytes 508

commit v2 on v1

--- a/solution.py
+++ b/solution.py
@@ -13,8 +13,7 @@
 PLANE = 9216
 BLK = 2304
 LANES = 128
-QUAD = 384
-CHUNK = 1152
+PART = 24
 MESH = pl.DeviceIdType.MESH
 
 hard_ratio = 0.3
@@ -29,10 +28,8 @@
     return lax.broadcasted_iota(jnp.int32, (rows, LANES), 1)
 
 
-def unpack_rows(value):
-    rows = value.shape[0]
-    lane = lane_id(rows)
-    a, b, c = value[:, 0:128], value[:, 128:256], value[:, 256:384]
+def unpack_rows(a, b, c):
+    lane = lane_id(a.shape[0])
     plain = (
         a,
         pltpu.roll(jnp.where(lane >= 96, a, b), 32, 1),
@@ -58,104 +55,123 @@
 
 
 def material_kernel(
-    depth, volume, in_dev,
+    depth, volume, in_dev, planes,
     sub_ref, pg_ref, pb_ref, p_ref, h_ref, b_ref, d_ref, g_ref, k_ref, y_ref,
     st_ref, pick_ref, sum_ref,
-    acc_ref, hist_ref,
+    acc_ref, hist_ref, wait_ref, dev_ref, del_ref, lev_ref, lev0_ref, tmp_ref,
 ):
     step = pl.program_id(0)
     group = lax.axis_index("rve")
     slab = lax.axis_index("slab")
     groups = pg_ref.shape[0]
-    per_block = BLK // CHUNK
-    quarter = step // per_block
     blocks_dev = 4 * depth
+    tiles = PLANE // LANES
+    parts = tuple(slice(t, t + PART) for t in range(0, tiles, PART))
+    quarter_rows = BLK // LANES
 
     @pl.when(step == 0)
     def _():
         acc_ref[...] = jnp.zeros_like(acc_ref)
 
-    zrow = lax.broadcasted_iota(jnp.int32, (depth, LANES), 0)
-    count = jnp.zeros((depth, LANES), jnp.int32)
-    turns = jnp.int32(1)
-    for z in range(depth):
-        n = sub_ref[group, slab * blocks_dev + z * 4 + quarter]
-        count = jnp.where(zrow == z, n, count)
-        turns = jnp.maximum(turns, n)
-    count = jnp.concatenate([count] * (QUAD // LANES), axis=1)
-    waiting = turns - count
-    inv = 1.0 / count.astype(jnp.float32)
-    waiting_f = waiting.astype(jnp.float32)
-
-    def dev_parts(ref, lanes, other=None):
-        parts = []
+    def dev_parts(ref, z, rows, other=None):
+        vals = []
         for c in range(6):
-            v = ref[c, 0, :, lanes]
+            v = ref[c, z, rows]
             if other is not None:
-                v = v - other[c, 0, :, lanes]
-            parts.append(v)
-        trace = parts[0] + parts[1] + parts[2]
+                v = v - other[c, z, rows]
+            vals.append(v)
+        trace = vals[0] + vals[1] + vals[2]
         third = trace * (1.0 / 3.0)
-        return [parts[c] - third if c < 3 else parts[c] for c in range(6)], trace
-
-    def sub_chunk(sc, _):
-        off = pl.multiple_of(sc * QUAD, QUAD)
-        lanes = pl.ds(off, QUAD)
-        dev0, tr0 = dev_parts(b_ref, lanes, p_ref)
-        devs, trs = dev_parts(d_ref, lanes)
-        mu = g_ref[0, :, lanes]
-        hard = h_ref[0, :, lanes]
-        delta = [devs[c] * inv for c in KEPT]
-        start = [dev0[c] - waiting_f * delta[i] for i, c in enumerate(KEPT)]
-        level0 = (11.0 * root_two_thirds / 2.2) * (y_ref[0, :, lanes] / mu + hard_ratio * hard)
-
-        def trial(dd):
-            dd = [dd[i] + delta[i] for i in range(5)]
-            square = (
-                2.0 * (dd[0] * (dd[0] + dd[1]) + dd[1] * dd[1])
-                + dd[2] * dd[2] + dd[3] * dd[3] + dd[4] * dd[4]
+        return [vals[c] - third if c < 3 else vals[c] for c in range(6)], trace
+
+    def trial(rows):
+        dd = [dev_ref[i, rows] + del_ref[i, rows] for i in range(5)]
+        square = (
+            2.0 * (dd[0] * (dd[0] + dd[1]) + dd[1] * dd[1])
+            + dd[2] * dd[2] + dd[3] * dd[3] + dd[4] * dd[4]
+        )
+        square = jnp.maximum(square, 1e-30)
+        return dd, square, lax.rsqrt(square)
+
+    def one_plane(z, _):
+        base = slab * blocks_dev + (step * planes + z) * 4
+        counts = [sub_ref[group, base + q] for q in range(4)]
+        turns = jnp.maximum(
+            jnp.maximum(counts[0], counts[1]), jnp.maximum(counts[2], counts[3])
+        )
+        for rows in parts:
+            row = lax.broadcasted_iota(jnp.int32, (PART, LANES), 0) + rows.start
+            count = jnp.full((PART, LANES), counts[0], jnp.int32)
+            for q in range(1, 4):
+                count = jnp.where(row >= q * quarter_rows, counts[q], count)
+            inv = 1.0 / count.astype(jnp.float32)
+            waiting = turns - count
+            wait_ref[rows] = waiting
+            waiting_f = waiting.astype(jnp.float32)
+            dev0, _ = dev_parts(b_ref, z, rows, p_ref)
+            devs, _ = dev_parts(d_ref, z, rows)
+            for i, c in enumerate(KEPT):
+                delta = devs[c] * inv
+                del_ref[i, rows] = delta
+                dev_ref[i, rows] = dev0[c] - waiting_f * delta
+            level0 = (11.0 * root_two_thirds / 2.2) * (
+                y_ref[z, rows] / g_ref[z, rows] + hard_ratio * h_ref[z, rows]
             )
-            square = jnp.maximum(square, 1e-30)
-            return dd, square, lax.rsqrt(square)
-
-        def substep(turn, carry):
-            dd, level = carry
-            dd, square, rs = trial(dd)
+            lev_ref[rows] = level0
+            lev0_ref[rows] = level0
+
+        def substep(turn, _):
+            for rows in parts:
+                dd, square, rs = trial(rows)
+                level = lev_ref[rows]
+                fac = jnp.minimum((1.0 + level * rs) * (1.0 / 11.0), 1.0)
+                fac = jnp.where(turn >= wait_ref[rows], fac, 1.0)
+                lev_ref[rows] = level + (1.0 - fac) * (square * rs)
+                for i in range(5):
+                    dev_ref[i, rows] = fac * dd[i]
+            return 0
+
+        lax.fori_loop(0, turns - 1, substep, 0)
+        sums = [None] * (8 + len(PAIRS))
+        for rows in parts:
+            dd, square, rs = trial(rows)
+            level = lev_ref[rows]
             fac = jnp.minimum((1.0 + level * rs) * (1.0 / 11.0), 1.0)
-            fac = jnp.where(turn >= waiting, fac, 1.0)
             level = level + (1.0 - fac) * (square * rs)
-            return tuple(fac * v for v in dd), level
-
-        dd, level = lax.fori_loop(0, turns - 1, substep, (tuple(start), level0))
-        dd, square, rs = trial(dd)
-        fac = jnp.minimum((1.0 + level * rs) * (1.0 / 11.0), 1.0)
-        level = level + (1.0 - fac) * (square * rs)
-        fin = [fac * v for v in dd]
-        coef = mu * fac
-        weight = (coef - mu) * (rs * rs)
-        bulk = k_ref[0, :, lanes]
-        vol = bulk * (tr0 + trs)
-        two_mu = 2.0 * mu
-        ms = [two_mu * v for v in fin]
-        wn = [weight * v for v in dd]
-        terms = [vol, bulk, coef] + ms + [wn[i] * dd[j] for i, j in PAIRS]
-        for t, v in enumerate(terms):
-            acc_ref[t] += v[:, 0:128] + v[:, 128:256] + v[:, 256:384]
-        ms6 = [ms[0], ms[1], -(ms[0] + ms[1]), ms[2], ms[3], ms[4]]
-        fin6 = [fin[0], fin[1], -(fin[0] + fin[1]), fin[2], fin[3], fin[4]]
-        fields = [ms6[c] + vol if c < 3 else ms6[c] for c in range(6)] + [coef]
-        row0 = (step * (CHUNK // QUAD) + sc) * 4
-        for f, v in enumerate(fields):
-            for r, rowv in enumerate(unpack_rows(v)):
-                for z0 in range(0, depth, 8):
-                    nz = min(8, depth - z0)
-                    st_ref[f, pl.ds(z0 * NVX + row0 + r, nz, stride=NVX), :] = rowv[z0 : z0 + nz]
-        for c in range(6):
-            hist_ref[c, :, lanes] = p_ref[c, 0, :, lanes] + (dev0[c] + devs[c] - fin6[c])
-        hist_ref[6, :, lanes] = hard + root_two_thirds * (level - level0)
+            fin = [fac * v for v in dd]
+            mu = g_ref[z, rows]
+            coef = mu * fac
+            weight = (coef - mu) * (rs * rs)
+            bulk = k_ref[z, rows]
+            dev0, tr0 = dev_parts(b_ref, z, rows, p_ref)
+            devs, trs = dev_parts(d_ref, z, rows)
+            vol = bulk * (tr0 + trs)
+            two_mu = 2.0 * mu
+            ms = [two_mu * v for v in fin]
+            wn = [weight * v for v in dd]
+            ms6 = [ms[0], ms[1], -(ms[0] + ms[1]), ms[2], ms[3], ms[4]]
+            fin6 = [fin[0], fin[1], -(fin[0] + fin[1]), fin[2], fin[3], fin[4]]
+            for c in range(6):
+                tmp_ref[c, rows] = ms6[c] + vol if c < 3 else ms6[c]
+                hist_ref[c, z, rows] = p_ref[c, z, rows] + (dev0[c] + devs[c] - fin6[c])
+            tmp_ref[6, rows] = coef
+            hist_ref[6, z, rows] = h_ref[z, rows] + root_two_thirds * (level - lev0_ref[rows])
+            terms = [vol, bulk, coef] + ms + [wn[i] * dd[j] for i, j in PAIRS]
+            for t, v in enumerate(terms):
+                for o in range(0, PART, 8):
+                    piece = v[o : o + 8]
+                    sums[t] = piece if sums[t] is None else sums[t] + piece
+        for t, v in enumerate(sums):
+            acc_ref[t] += v
+
+        for f in range(7):
+            for g8 in range(tiles // 24):
+                a, b, c = (tmp_ref[f, pl.ds(24 * g8 + k, 8, stride=3)] for k in range(3))
+                for r, rowv in enumerate(unpack_rows(a, b, c)):
+                    st_ref[f, z, pl.ds(32 * g8 + r, 8, stride=4)] = rowv
         return 0
 
-    lax.fori_loop(0, CHUNK // QUAD, sub_chunk, 0)
+    lax.fori_loop(0, planes, one_plane, 0)
 
     for g in range(groups):
         chosen = jnp.int32(0)
@@ -164,13 +180,16 @@
             chosen = jnp.where(
                 pg_ref[g, slot] == group, pb_ref[g, slot] - slab * blocks_dev, chosen
             )
-
-        @pl.when(chosen % 4 == quarter)
+        z = chosen // 4 - step * planes
+
+        @pl.when((z >= 0) & (z < planes))
         def _():
-            z = chosen // 4
-            lanes = pl.ds(pl.multiple_of((step % per_block) * CHUNK, CHUNK), CHUNK)
-            for c in range(7):
-                pick_ref[g, pl.ds(c, 1), lanes] = hist_ref[c, pl.ds(z, 1), :]
+            for q in range(4):
+
+                @pl.when(chosen % 4 == q)
+                def _():
+                    for c in range(7):
+                        pick_ref[g, c] = hist_ref[c, z, q * quarter_rows : (q + 1) * quarter_rows]
 
     @pl.when(step == pl.num_programs(0) - 1)
     def _():
@@ -259,8 +278,6 @@
         move.start()
         moves.append(move)
 
-    c8[0] = jnp.zeros((NVX, LANES), jnp.float32)
-
     def own_planes(z, _):
         c8[z + 1] = st_ref[6, z] * 0.125
         return 0
@@ -429,19 +446,17 @@
 
     lax.fori_loop(0, depth, last_turn, 0)
 
-    def to_flat(j, _):
+    def to_flat(z, _):
         for c in range(3):
-            for z0 in range(0, depth, 8):
-                nz = min(8, depth - z0)
+            for g8 in range(NVX // 32):
                 rows4 = [
-                    uu[c, pl.ds(z0 * NVX + 4 * j + r, nz, stride=NVX), :] for r in range(4)
+                    uu[c, pl.ds(z * NVX + 32 * g8 + r, 8, stride=4), :] for r in range(4)
                 ]
                 for t, v in enumerate(pack_rows(rows4)):
-                    off = pl.multiple_of(j * QUAD + t * LANES, LANES)
-                    out_ref[c, 0, pl.ds(z0, nz), pl.ds(off, LANES)] = v
+                    out_ref[c, z, pl.ds(24 * g8 + t, 8, stride=3)] = v
         return 0
 
-    lax.fori_loop(0, PLANE // QUAD, to_flat, 0)
+    lax.fori_loop(0, depth, to_flat, 0)
 
     for move in moves:
         move.wait()
@@ -449,7 +464,7 @@
         source = pg_ref[group, slab * in_dev + j]
         got = ab[source]
         for c in range(7):
-            inbox_ref[c, 0, pl.ds(j, 1), :] = got[c : c + 1]
+            inbox_ref[c, pl.ds(j, BLK // LANES, stride=in_dev), :] = got[c]
     for copy in element:
         copy.wait()
     mine = jnp.zeros((1, LANES), jnp.float32)
@@ -469,32 +484,51 @@
     smem = pl.BlockSpec(memory_space=pltpu.SMEM)
     vmem = pl.BlockSpec(memory_space=pltpu.VMEM)
     f32 = jnp.float32
-    six = pl.BlockSpec((6, 1, depth, CHUNK), lambda i: (0, 0, 0, i))
-    one = pl.BlockSpec((1, depth, CHUNK), lambda i: (0, 0, i))
+    tiles = PLANE // LANES
+    planes = depth // 4 if depth % 4 == 0 else 1
+    six = pl.BlockSpec((6, planes, tiles, LANES), lambda i: (0, i, 0, 0))
+    one = pl.BlockSpec((planes, tiles, LANES), lambda i: (i, 0, 0))
 
     def whole(shape):
         return pl.BlockSpec(shape, lambda i: (0,) * len(shape))
 
-    shapes = ((7, depth * NVX, LANES), (groups, 7, BLK), (1, LANES))
+    def view6(x):
+        return x.reshape(6, depth, tiles, LANES)
+
+    def view1(x):
+        return x.reshape(depth, tiles, LANES)
+
+    pick_shape = (groups, 7, BLK // LANES, LANES)
+    shapes = ((7, depth, NVX, LANES), pick_shape, (1, LANES))
     stress, picked, partial_sums = pl.pallas_call(
-        functools.partial(material_kernel, depth, volume, in_dev),
-        grid=(PLANE // CHUNK,),
+        functools.partial(material_kernel, depth, volume, in_dev, planes),
+        grid=(depth // planes,),
         in_specs=[smem, smem, smem, six, one, six, six, one, one, one],
-        out_specs=[whole(s) for s in shapes],
+        out_specs=[
+            pl.BlockSpec((7, planes, NVX, LANES), lambda i: (0, i, 0, 0)),
+            whole(shapes[1]),
+            whole(shapes[2]),
+        ],
         out_shape=[jax.ShapeDtypeStruct(s, f32) for s in shapes],
         scratch_shapes=[
-            pltpu.VMEM((8 + len(PAIRS), depth, LANES), f32),
-            pltpu.VMEM((7, depth, CHUNK), f32),
+            pltpu.VMEM((8 + len(PAIRS), 8, LANES), f32),
+            pltpu.VMEM((7, planes, tiles, LANES), f32),
+            pltpu.VMEM((tiles, LANES), jnp.int32),
+            pltpu.VMEM((5, tiles, LANES), f32),
+            pltpu.VMEM((5, tiles, LANES), f32),
+            pltpu.VMEM((tiles, LANES), f32),
+            pltpu.VMEM((tiles, LANES), f32),
+            pltpu.VMEM((7, tiles, LANES), f32),
         ],
         compiler_params=pltpu.CompilerParams(
-            dimension_semantics=("arbitrary",), vmem_limit_bytes=48 * 1024 * 1024
+            dimension_semantics=("arbitrary",), vmem_limit_bytes=16 * 1024 * 1024
         ),
         name="material",
     )(
-        substeps, pull_group, pull_block, plastic_strain, hardening_var, strain_start,
-        strain_step, shear_mod, bulk_mod, yield_stress,
+        substeps, pull_group, pull_block, view6(plastic_strain), view1(hardening_var),
+        view6(strain_start), view6(strain_step), view1(shear_mod), view1(bulk_mod),
+        view1(yield_stress),
     )
-    stress = stress.reshape(7, depth, NVX, LANES)
     plane = (NVX, LANES)
     dma = pltpu.SemaphoreType.DMA
     correction, inbox, element_sums = pl.pallas_call(
@@ -502,8 +536,8 @@
         in_specs=[smem, smem, vmem, vmem, vmem],
         out_specs=[vmem, vmem, vmem],
         out_shape=[
-            jax.ShapeDtypeStruct((3, 1, depth, PLANE), f32),
-            jax.ShapeDtypeStruct((7, 1, in_dev, BLK), f32),
+            jax.ShapeDtypeStruct((3, depth, tiles, LANES), f32),
+            jax.ShapeDtypeStruct((7, in_dev * BLK // LANES, LANES), f32),
             jax.ShapeDtypeStruct((1, 42), f32),
         ],
         scratch_shapes=[
@@ -518,7 +552,7 @@
             pltpu.VMEM((ITERS - 1, 2, 3) + plane, f32),
             pltpu.VMEM((ITERS, 8, LANES), f32),
             pltpu.VMEM((ITERS, slabs, 8, LANES), f32),
-            pltpu.VMEM((groups, 7, BLK), f32),
+            pltpu.VMEM(pick_shape, f32),
             pltpu.VMEM((groups, 8, LANES), f32),
             pltpu.VMEM((8, LANES), f32),
             dma((ITERS + 1, 2)),
@@ -531,11 +565,13 @@
             dma((groups,)),
         ],
         compiler_params=pltpu.CompilerParams(
-            collective_id=0, has_side_effects=True, vmem_limit_bytes=60 * 1024 * 1024
+            collective_id=0, has_side_effects=True, vmem_limit_bytes=26 * 1024 * 1024
         ),
         name="solve",
     )(pull_group, owner, stress, picked, partial_sums)
-    return correction, inbox, element_sums
+    correction = correction.reshape(3, 1, depth, PLANE)
+    inbox = inbox.reshape(7, BLK // LANES, in_dev, LANES).swapaxes(1, 2)
+    return correction, inbox.reshape(7, 1, in_dev, BLK), element_sums
 
 
 def solution(mesh):

time: 107 us -> 93.8 us (0.88)
  Pallas kernels: 88.6 us -> 79 us
  local copies, waits for them, and re-layouts: 16.5 us -> 13.7 us
    pallas_call x1, Pallas kernels: 20.7 us -> 14.4 us  [on_device(): pl.pallas_call(functools.partial(material_kernel, depth, volume, in_dev,...]
    pallas_call x1 -> x0, local copies, waits for them, and re-layouts: 3.94 us -> none  [on_device(): pl.pallas_call(functools.partial(solve_kernel, depth, groups, slabs, in_d...]
    pallas_call x1, Pallas kernels: 68 us -> 64.6 us  [on_device(): pl.pallas_call(functools.partial(solve_kernel, depth, groups, slabs, in_d...]
    unnamed x31 -> x26, local copies, waits for them, and re-layouts: 12.5 us -> 12.9 us
where the time goes in v2:
time: 93.8 us; the launch traced here: 93.4 us
  Pallas kernels  79 us (84%)
  local copies, waits for them, and re-layouts  13.7 us (15%)
    pallas_call x1, Pallas kernels, on_device(): pl.pallas_call(functools.partial(solve_kernel, depth, groups, slabs, in_d...  64.6 us
    pallas_call x1, Pallas kernels, on_device(): pl.pallas_call(functools.partial(material_kernel, depth, volume, in_dev,...  14.4 us
    unnamed x26, local copies, waits for them, and re-layouts  12.9 us

profile of v2, /device:TPU:0, one launch (start us, length us, event | category | flops | bytes accessed | tf_op | source)
XLA Modules:
  0.0 93.4 jit_solution(4763498935256988123)
XLA Ops:
  0.6 0.0 copy-start
  0.6 1.7 %copy-done = f32[6,1,12,9216]{3,1,2,0:T(1,128)S(1)} copy-done((f32[6,1,12,9216]{3,1,2,0:T(1,128)S(1)}, f32[6,1,12,9216]{3,1,2,0:T(1,128)}, u32[]{:S(2)}) %copy-start) | copy-done | bytes 2654232
  2.4 0.0 copy-start.1
  2.4 1.7 %copy-done.1 = f32[6,1,12,9216]{3,1,2,0:T(1,128)S(1)} copy-done((f32[6,1,12,9216]{3,1,2,0:T(1,128)S(1)}, f32[6,1,12,9216]{3,1,2,0:T(1,128)}, u32[]{:S(2)}) %copy-start.1) | copy-done | bytes 2654232
  4.1 0.0 copy-start.2
  4.1 1.7 %copy-done.2 = f32[6,1,12,9216]{3,1,2,0:T(1,128)S(1)} copy-done((f32[6,1,12,9216]{3,1,2,0:T(1,128)S(1)}, f32[6,1,12,9216]{3,1,2,0:T(1,128)}, u32[]{:S(2)}) %copy-start.2) | copy-done | bytes 2654232
  5.9 0.0 copy-start.3
  5.9 1.0 %copy-done.3 = f32[1,12,9216]{2,0,1:T(1,128)S(1)} copy-done((f32[1,12,9216]{2,0,1:T(1,128)S(1)}, f32[1,12,9216]{2,0,1:T(1,128)}, u32[]{:S(2)}) %copy-start.3) | copy-done | bytes 442392
  6.9 0.0 copy-start.4
  6.9 1.0 %copy-done.4 = f32[1,12,9216]{2,0,1:T(1,128)S(1)} copy-done((f32[1,12,9216]{2,0,1:T(1,128)S(1)}, f32[1,12,9216]{2,0,1:T(1,128)}, u32[]{:S(2)}) %copy-start.4) | copy-done | bytes 442392
  7.9 0.0 copy-start.5
  7.9 1.0 %copy-done.5 = f32[1,12,9216]{2,0,1:T(1,128)S(1)} copy-done((f32[1,12,9216]{2,0,1:T(1,128)S(1)}, f32[1,12,9216]{2,0,1:T(1,128)}, u32[]{:S(2)}) %copy-start.5) | copy-done | bytes 442392
  8.9 1.0 %copy-done.6 = f32[1,12,9216]{2,0,1:T(1,128)S(1)} copy-done((f32[1,12,9216]{2,0,1:T(1,128)S(1)}, f32[1,12,9216]{2,0,1:T(1,128)}, u32[]{:S(2)}) %copy-start.6) | copy-done | bytes 442392
  9.9 0.7 copy-done.7
  10.6 0.7 copy-done.9
  11.3 0.7 copy-done.10
  12.0 14.4 %material.1 = (f32[7,12,96,128]{3,2,1,0:T(8,128)S(1)}, f32[4,7,18,128]{3,2,1,0:T(8,128)S(1)}, f32[1,128]{1,0:T(1,128)S(1)}) custom-call(s32[4,384]{1,0:T(4,128)S(1)} %copy-done.9, s32[4,16]{1,0:T(4,128)S(1)} %copy-done.7, s32[4,16]{1,0:T(4,128)S(1)} %copy-done.10, f32[6,12,72,128]{3,2,1,0:T(8,128)S(1)} %bitcast.12, f32[12,72,128]{2,1,0:T(8,128)S(1)} %bitcast.16, ...), custom_call_target="tpu_custom_call" | custom-call | tf_op jit(solution)/shard_map/material/pallas_call | solution.py:503
  26.4 0.0 copy-done.8
  26.4 0.0 copy-done.11
  26.4 64.6 %solve.1 = (f32[3,12,72,128]{3,2,1,0:T(8,128)S(1)}, f32[7,36,128]{2,1,0:T(8,128)S(1)}, f32[1,42]{1,0:T(1,128)S(1)}) custom-call(s32[4,16]{1,0:T(4,128)S(1)} %copy-done.8, s32[4]{0:T(128)S(1)} %copy-done.11, f32[7,12,96,128]{3,2,1,0:T(8,128)S(1)} %get-tuple-element.9.st_ref, f32[4,7,18,128]{3,2,1,0:T(8,128)S(1)} %get-tuple-element.10.pick_ref, ...), custom_call_target="tpu_custom_call" | custom-call | tf_op jit(solution)/shard_map/solve/pallas_call | solution.py:534
  91.0 0.1 reshape.44
  91.1 0.7 reshape.45
  91.8 1.1 %copy.23 = f32[3,1,12,9216]{3,1,2,0:T(1,128)} copy(f32[3,1,12,9216]{3,1,2,0:T(1,128)S(1)} %bitcast.15) | data formatting | bytes 2654208
  92.9 0.5 copy.24
  (7 shorter events, 0.0 us)
Async XLA Ops:
  0.6 1.8 %copy-start = (f32[6,1,12,9216]{3,1,2,0:T(1,128)S(1)}, f32[6,1,12,9216]{3,1,2,0:T(1,128)}, u32[]{:S(2)}) copy-start(f32[6,1,12,9216]{3,1,2,0:T(1,128)} %param.11) | copy-start | bytes 7962628
  2.4 1.7 %copy-start.1 = (f32[6,1,12,9216]{3,1,2,0:T(1,128)S(1)}, f32[6,1,12,9216]{3,1,2,0:T(1,128)}, u32[]{:S(2)}) copy-start(f32[6,1,12,9216]{3,1,2,0:T(1,128)} %param.13) | copy-start | bytes 7962628
  4.1 1.7 %copy-start.2 = (f32[6,1,12,9216]{3,1,2,0:T(1,128)S(1)}, f32[6,1,12,9216]{3,1,2,0:T(1,128)}, u32[]{:S(2)}) copy-start(f32[6,1,12,9216]{3,1,2,0:T(1,128)} %param.14) | copy-start | bytes 7962628
  5.9 1.0 %copy-start.3 = (f32[1,12,9216]{2,0,1:T(1,128)S(1)}, f32[1,12,9216]{2,0,1:T(1,128)}, u32[]{:S(2)}) copy-start(f32[1,12,9216]{2,0,1:T(1,128)} %param.12) | copy-start | bytes 1327108
  6.9 1.0 %copy-start.4 = (f32[1,12,9216]{2,0,1:T(1,128)S(1)}, f32[1,12,9216]{2,0,1:T(1,128)}, u32[]{:S(2)}) copy-start(f32[1,12,9216]{2,0,1:T(1,128)} %param.15) | copy-start | bytes 1327108
  7.9 1.0 %copy-start.5 = (f32[1,12,9216]{2,0,1:T(1,128)S(1)}, f32[1,12,9216]{2,0,1:T(1,128)}, u32[]{:S(2)}) copy-start(f32[1,12,9216]{2,0,1:T(1,128)} %param.16) | copy-start | bytes 1327108
  8.9 1.0 %copy-start.6 = (f32[1,12,9216]{2,0,1:T(1,128)S(1)}, f32[1,12,9216]{2,0,1:T(1,128)}, u32[]{:S(2)}) copy-start(f32[1,12,9216]{2,0,1:T(1,128)} %param.17) | copy-start | bytes 1327108
  9.9 0.7 copy-start.7
  10.6 0.7 copy-start.9
  11.3 0.7 copy-start.10
  12.0 14.4 %copy-start.8 = (s32[4,16]{1,0:T(4,128)S(1)}, s32[4,16]{1,0:T(4,128)}, u32[]{:S(2)}) copy-start(s32[4,16]{1,0:T(4,128)} %pg_ref.3) | copy-start | bytes 772
  12.0 14.4 %copy-start.11 = (s32[4]{0:T(128)S(1)}, s32[4]{0:T(128)}, u32[]{:S(2)}) copy-start(s32[4]{0:T(128)} %own_ref.1) | copy-start | bytes 52

commit v3 on v2

--- a/solution.py
+++ b/solution.py
@@ -223,18 +223,27 @@
         sum_ref[...] = row
 
 
-def spread(v):
-    p = v + pltpu.roll(v, NVX - 1, 0)
-    p = p + pltpu.roll(p, 1, 0)
-    q = p + pltpu.roll(p, LANES - 1, 1)
-    return q + pltpu.roll(q, 1, 1)
-
-
-def fold(v):
-    out = v[0:8]
-    for i in range(1, NVX // 8):
-        out = out + v[8 * i : 8 * i + 8]
-    return out
+def ring_next(pieces, sub):
+    turned = [pltpu.roll(p, 7, 0) for p in pieces]
+    count = len(pieces)
+    return [jnp.where(sub < 7, turned[i], turned[(i + 1) % count]) for i in range(count)]
+
+
+def ring_prev(pieces, sub):
+    turned = [pltpu.roll(p, 1, 0) for p in pieces]
+    count = len(pieces)
+    return [jnp.where(sub > 0, turned[i], turned[i - 1]) for i in range(count)]
+
+
+def cut(v):
+    return [v[i : i + 8] for i in range(0, NVX, 8)]
+
+
+def spread(pieces, sub):
+    p = [x + y for x, y in zip(pieces, ring_next(pieces, sub))]
+    p = [x + y for x, y in zip(p, ring_prev(p, sub))]
+    q = [x + pltpu.roll(x, LANES - 1, 1) for x in p]
+    return [x + pltpu.roll(x, 1, 1) for x in q]
 
 
 def solve_kernel(
@@ -285,8 +294,12 @@
     lax.fori_loop(0, depth, own_planes, 0)
     ab[group] = pick_ref[group]
 
+    sub = lax.broadcasted_iota(jnp.int32, (8, LANES), 0)
+
     def ydiff(v):
-        return pltpu.roll(v, NVX - 1, 0) - pltpu.roll(v, 1, 0)
+        v = cut(v)
+        both = [x - y for x, y in zip(ring_next(v, sub), ring_prev(v, sub))]
+        return jnp.concatenate(both, axis=0)
 
     def xdiff(v):
         return pltpu.roll(v, LANES - 1, 1) - pltpu.roll(v, 1, 1)
@@ -318,7 +331,10 @@
     c8[depth + 1] = sh[1, 6] * 0.125
 
     def diagonal(z, _):
-        ee[z] = 8.0 * (8.0 + mass_weight) * c8[z] + spread(c8[z - 1] + 2.0 * c8[z] + c8[z + 1])
+        wide = spread(cut(c8[z - 1] + 2.0 * c8[z] + c8[z + 1]), sub)
+        for i, w in enumerate(wide):
+            at = slice(8 * i, 8 * i + 8)
+            ee[z, at] = 8.0 * (8.0 + mass_weight) * c8[z, at] + w
         return 0
 
     lax.fori_loop(1, depth + 1, diagonal, 0)
@@ -327,17 +343,23 @@
 
     def apply_plane(z, carry):
         norm, curve = carry
-        ca, cb, cc = c8[z - 1], c8[z], c8[z + 1]
-        diag = ee[z]
         for c in range(3):
-            ra, rb, rc = rr[c, z - 1], rr[c, z], rr[c, z + 1]
-            crb = cb * rb
-            plain = spread((ra + rc) + (rb + rb))
-            mixed = spread((ca * ra + cc * rc) + (crb + crb))
-            image = diag * rb - cb * plain - mixed
-            im[c, z] = image
-            norm = norm + fold(rb * rb)
-            curve = curve + fold(rb * image)
+            plain, mixed = [], []
+            for i in range(0, NVX, 8):
+                at = slice(i, i + 8)
+                ra, rb, rc = rr[c, z - 1, at], rr[c, z, at], rr[c, z + 1, at]
+                crb = c8[z, at] * rb
+                plain.append((ra + rc) + (rb + rb))
+                mixed.append((c8[z - 1, at] * ra + c8[z + 1, at] * rc) + (crb + crb))
+            plain = spread(plain, sub)
+            mixed = spread(mixed, sub)
+            for i in range(0, NVX, 8):
+                at = slice(i, i + 8)
+                rb = rr[c, z, at]
+                image = ee[z, at] * rb - c8[z, at] * plain[i // 8] - mixed[i // 8]
+                im[c, z, at] = image
+                norm = norm + rb * rb
+                curve = curve + rb * image
         return norm, curve
 
     def reduce_start(it, norm, curve, extra):
@@ -492,11 +514,14 @@
     def whole(shape):
         return pl.BlockSpec(shape, lambda i: (0,) * len(shape))
 
+    def stay(x):
+        return pltpu.with_memory_space_constraint(x, pltpu.HBM)
+
     def view6(x):
-        return x.reshape(6, depth, tiles, LANES)
+        return stay(x.reshape(6, depth, tiles, LANES))
 
     def view1(x):
-        return x.reshape(depth, tiles, LANES)
+        return stay(x.reshape(depth, tiles, LANES))
 
     pick_shape = (groups, 7, BLK // LANES, LANES)
     shapes = ((7, depth, NVX, LANES), pick_shape, (1, LANES))

time: 93.8 us -> 83.8 us (0.89)
  local copies, waits for them, and re-layouts: 13.7 us -> 4.44 us
    unnamed x26 -> x12, local copies, waits for them, and re-layouts: 12.9 us -> 3.63 us
where the time goes in v3:
time: 83.8 us; the launch traced here: 83.5 us
  Pallas kernels  78.4 us (94%)
  local copies, waits for them, and re-layouts  4.44 us (5%)
    pallas_call x1, Pallas kernels, on_device(): pl.pallas_call(functools.partial(solve_kernel, depth, groups, slabs, in_d...  63.9 us
    pallas_call x1, Pallas kernels, on_device(): pl.pallas_call(functools.partial(material_kernel, depth, volume, in_dev,...  14.5 us
    unnamed x12, local copies, waits for them, and re-layouts  3.63 us

profile of v3, /device:TPU:0, one launch (start us, length us, event | category | flops | bytes accessed | tf_op | source)
XLA Modules:
  0.0 83.5 jit_solution(8556261807485264828)
XLA Ops:
  0.6 0.0 copy-start
  0.6 0.7 copy-done
  1.3 0.0 copy-start.2
  1.3 0.7 copy-done.2
  2.0 0.0 copy-start.3
  2.0 0.7 copy-done.3
  2.7 0.0 copy-start.1
  2.7 0.0 copy-start.4
  2.7 14.5 %material.1 = (f32[7,12,96,128]{3,2,1,0:T(8,128)S(1)}, f32[4,7,18,128]{3,2,1,0:T(8,128)S(1)}, f32[1,128]{1,0:T(1,128)S(1)}) custom-call(s32[4,384]{1,0:T(4,128)S(1)} %copy-done.2, s32[4,16]{1,0:T(4,128)S(1)} %copy-done, s32[4,16]{1,0:T(4,128)S(1)} %copy-done.3, f32[6,12,72,128]{3,2,1,0:T(8,128)} %bitcast.13, f32[12,72,128]{2,1,0:T(8,128)} %bitcast.17, ...), custom_call_target="tpu_custom_call" | custom-call | tf_op jit(solution)/shard_map/material/pallas_call | solution.py:528
  17.2 0.0 copy-done.1
  17.2 0.0 copy-done.4
  17.2 63.9 %solve.1 = (f32[3,12,72,128]{3,2,1,0:T(8,128)S(1)}, f32[7,36,128]{2,1,0:T(8,128)S(1)}, f32[1,42]{1,0:T(1,128)S(1)}) custom-call(s32[4,16]{1,0:T(4,128)S(1)} %copy-done.1, s32[4]{0:T(128)S(1)} %copy-done.4, f32[7,12,96,128]{3,2,1,0:T(8,128)S(1)} %get-tuple-element.9.st_ref, f32[4,7,18,128]{3,2,1,0:T(8,128)S(1)} %get-tuple-element.10.pick_ref, ...), custom_call_target="tpu_custom_call" | custom-call | tf_op jit(solution)/shard_map/solve/pallas_call | solution.py:559
  81.1 0.1 reshape.44
  81.3 0.7 reshape.45
  82.0 1.1 %copy.23 = f32[3,1,12,9216]{3,1,2,0:T(1,128)} copy(f32[3,1,12,9216]{3,1,2,0:T(1,128)S(1)} %bitcast.12) | data formatting | bytes 2654208
  83.0 0.5 copy.24
  (1 shorter events, 0.0 us)
Async XLA Ops:
  0.6 0.7 copy-start
  1.3 0.7 copy-start.2
  2.0 0.7 copy-start.3
  2.7 14.5 %copy-start.1 = (s32[4,16]{1,0:T(4,128)S(1)}, s32[4,16]{1,0:T(4,128)}, u32[]{:S(2)}) copy-start(s32[4,16]{1,0:T(4,128)} %pg_ref.3) | copy-start | bytes 772
  2.7 14.5 %copy-start.4 = (s32[4]{0:T(128)S(1)}, s32[4]{0:T(128)}, u32[]{:S(2)}) copy-start(s32[4]{0:T(128)} %own_ref.1) | copy-start | bytes 52
